TPU v7x, 32 devices: a whole 2x2x4 slice. The times are simulated.
32 devices in a mesh: groups: 2 (over y), ctx: 4 (over z), mp: 4 (over x, core).
Axes of the slice: x: 2, y: 2, z: 4, core: 2. Of those that a mesh axis runs over, the one named last changes fastest.
Arguments:
- block_entry_input: bfloat16 [1536, 2048], P('mp', ('groups', 'ctx')), parts along dimension 1, may hold values from -6 to 6
- first_conv_taps: bfloat16 [3, 768, 1536], P(None, 'mp'), may hold values from -0.09375 to 0.09375
- first_pointwise_weight: bfloat16 [1536, 768], P(None, 'mp'), may hold values from -0.21875 to 0.21875
- second_conv_taps: bfloat16 [3, 768, 1536], P(None, 'mp'), may hold values from -0.09375 to 0.09375
- second_pointwise_weight: bfloat16 [1536, 768], P(None, 'mp'), may hold values from -0.21875 to 0.21875
- grad_heads: bfloat16 [8, 192, 2048], P('mp', 'ctx', 'groups'), parts along dimension 2, may hold values from -6 to 6
Outputs:
- second_block_output: bfloat16 [1536, 2048], P('mp', ('groups', 'ctx')), parts along dimension 1
- entry_input_gradient: bfloat16 [1536, 2048], P('mp', ('groups', 'ctx')), parts along dimension 1
- first_taps_gradient: float32 [6, 768, 1536], P('groups', 'mp', 'ctx'), parts along dimension 0
- first_projection_gradient: float32 [3072, 768], P(('groups', 'ctx'), 'mp'), parts along dimension 0
- second_taps_gradient: float32 [6, 768, 1536], P('groups', 'mp', 'ctx'), parts along dimension 0
- second_projection_gradient: float32 [3072, 768], P(('groups', 'ctx'), 'mp'), parts along dimension 0
There are 2 independent parts, one for each index of `groups`. A program takes and returns all parts, laid end to end along the dimension named above; an argument that names none is the same for every part. Nothing has to cross between parts.
All inputs are finite; a program needn't handle non-finite values.
Results may differ from a plain program's by a relative error of at most 0.034.
Values may be sent and summed in bfloat16 or wider, within the bound.
No kernel may reach another device: no remote copies, remote signals or barrier semaphores. Data moves between devices by JAX's collectives and lax.ppermute only.
A program may use at most 192 MiB of HBM per device.

v0:
```python
import jax
import jax.numpy as jnp
from jax import lax
from jax.sharding import PartitionSpec as P

FIRST_DILATION = 1024
SECOND_DILATION = 2048


def shifted(value, axis, by):
    length = lax.axis_size(axis)
    pairs = [(i, i + by) for i in range(length) if 0 <= i + by < length]
    return lax.ppermute(value, axis, pairs)


def gelu_slope(values):
    return jax.jvp(jax.nn.gelu, (values,), (jnp.ones_like(values),))[1]


def contract_first(left, right):
    return lax.dot_general(
        left, right, (((0,), (0,)), ((), ())), preferred_element_type=jnp.float32
    )


def contract_last(left, right):
    return lax.dot_general(
        left, right, (((1,), (1,)), ((), ())), preferred_element_type=jnp.float32
    )


def hop_steps(activations, dilation):
    return dilation // activations.shape[1]


def residual_block_forward(activations, conv_weight, point_weight, dilation):
    hop_count = hop_steps(activations, dilation)
    squash_part = jax.nn.gelu(activations.astype(jnp.float32)).astype(jnp.bfloat16)
    squashed = lax.all_gather(squash_part, "mp", axis=0, tiled=True)
    earlier = shifted(squashed, "ctx", hop_count)
    later = shifted(squashed, "ctx", -hop_count)
    pre_act = jnp.dot(conv_weight[0], earlier, preferred_element_type=jnp.float32)
    pre_act = pre_act + jnp.dot(conv_weight[1], squashed, preferred_element_type=jnp.float32)
    pre_act = pre_act + jnp.dot(conv_weight[2], later, preferred_element_type=jnp.float32)
    hidden = jax.nn.gelu(pre_act).astype(jnp.bfloat16)
    mixed = lax.psum_scatter(
        jnp.dot(point_weight, hidden, preferred_element_type=jnp.float32).astype(jnp.bfloat16),
        "mp",
        scatter_dimension=0,
        tiled=True,
    ).astype(jnp.float32)
    result = (activations.astype(jnp.float32) + mixed).astype(jnp.bfloat16)
    return (result, squashed, pre_act, hidden)


def residual_block_backward(
    incoming_gradient, activations, squashed, pre_act, hidden, conv_weight, point_weight, dilation
):
    hop_count = hop_steps(activations, dilation)
    upstream_full = lax.all_gather(incoming_gradient, "mp", axis=0, tiled=True)
    grad_hidden = contract_first(point_weight, upstream_full)
    grad_pre = (grad_hidden * gelu_slope(pre_act)).astype(jnp.bfloat16)
    grad_later = shifted(grad_pre, "ctx", -hop_count)
    grad_earlier = shifted(grad_pre, "ctx", hop_count)
    moved = (grad_later, grad_pre, grad_earlier)
    grad_conv = jnp.stack(
        [
            contract_last(moved[0], squashed),
            contract_last(moved[1], squashed),
            contract_last(moved[2], squashed),
        ]
    )
    grad_point = contract_last(upstream_full, hidden)
    total = contract_first(conv_weight[0], moved[0])
    total = total + contract_first(conv_weight[1], moved[1])
    grad_squash = lax.psum_scatter(
        (total + contract_first(conv_weight[2], moved[2])).astype(jnp.bfloat16),
        "mp",
        scatter_dimension=0,
        tiled=True,
    ).astype(jnp.float32)
    previous = (
        incoming_gradient.astype(jnp.float32)
        + grad_squash * gelu_slope(activations.astype(jnp.float32))
    ).astype(jnp.bfloat16)
    return (previous, grad_conv, grad_point)


def reduce_block(grad_conv, grad_point):
    return (
        lax.psum_scatter(
            grad_conv.astype(jnp.bfloat16), "ctx", scatter_dimension=2, tiled=True
        ).astype(jnp.float32),
        lax.psum_scatter(
            grad_point.astype(jnp.bfloat16), "ctx", scatter_dimension=0, tiled=True
        ).astype(jnp.float32),
    )


def shards(
    block_entry_input,
    first_conv_taps,
    first_pointwise_weight,
    second_conv_taps,
    second_pointwise_weight,
    grad_heads,
):
    regrouped = lax.all_to_all(grad_heads, "ctx", split_axis=2, concat_axis=1, tiled=True)
    incoming_gradient = regrouped.reshape(
        regrouped.shape[0] * regrouped.shape[1], regrouped.shape[2]
    )
    between_blocks_state, first_gelu_output, first_preactivation, first_hidden_state = (
        residual_block_forward(
            block_entry_input, first_conv_taps, first_pointwise_weight, FIRST_DILATION
        )
    )
    second_block_output, second_gelu_output, second_preactivation, second_hidden_state = (
        residual_block_forward(
            between_blocks_state, second_conv_taps, second_pointwise_weight, SECOND_DILATION
        )
    )
    incoming_gradient, conv_grad_b, point_grad_b = residual_block_backward(
        incoming_gradient,
        between_blocks_state,
        second_gelu_output,
        second_preactivation,
        second_hidden_state,
        second_conv_taps,
        second_pointwise_weight,
        SECOND_DILATION,
    )
    conv_grad_b, point_grad_b = reduce_block(conv_grad_b, point_grad_b)
    entry_input_gradient, conv_grad_a, point_grad_a = residual_block_backward(
        incoming_gradient,
        block_entry_input,
        first_gelu_output,
        first_preactivation,
        first_hidden_state,
        first_conv_taps,
        first_pointwise_weight,
        FIRST_DILATION,
    )
    conv_grad_a, point_grad_a = reduce_block(conv_grad_a, point_grad_a)
    return (
        second_block_output,
        entry_input_gradient,
        conv_grad_a,
        point_grad_a,
        conv_grad_b,
        point_grad_b,
    )


def solution(mesh):
    placed = (
        P("mp", ("groups", "ctx")),
        P(None, "mp", None),
        P(None, "mp"),
        P(None, "mp", None),
        P(None, "mp"),
        P("mp", "ctx", "groups"),
    )
    return jax.shard_map(
        shards,
        mesh=mesh,
        in_specs=placed,
        out_specs=(
            P("mp", ("groups", "ctx")),
            P("mp", ("groups", "ctx")),
            P("groups", "mp", "ctx"),
            P(("groups", "ctx"), "mp"),
            P("groups", "mp", "ctx"),
            P(("groups", "ctx"), "mp"),
        ),
        check_vma=False,
    )
```

profile of v0, /device:TPU:0, one launch (start us, length us, event | category | flops | bytes accessed | tf_op | source)
XLA Modules:
  0.0 296.0 jit_solution(17952154528425579025)
XLA Ops:
  7.2 1.2 fusion.62
  8.5 10.0 %all_gather.12 = bf16[1536,256]{1,0:T(8,128)(2,1)S(1)} all-gather(bf16[384,256]{1,0:T(8,128)(2,1)S(1)} %fusion.62), channel_id=1, replica_groups=mesh['groups'=2,'ctx'=4,'mp'=4] {'mp'}, dimensions={0}, use_global_device_ids=true | all-gather | bytes 983040 | tf_op jit(solution)/shard_map/all_gather | solution.py:39
  19.2 1.4 fusion.33
  22.1 1.2 copy.33
  23.3 24.3 %reduce-scatter.25.cloned.1.call-done = bf16[384,256]{1,0:T(8,128)(2,1)} async-done(((bf16[1536,256]{1,0:T(8,128)(2,1)}), bf16[384,256]{1,0:T(8,128)(2,1)}) %reduce-scatter.25.cloned.1.call-update) | async-done | bytes 196624 | tf_op jit(solution)/shard_map/reduce_scatter | solution.py:46
  47.6 1.1 fusion.71
  48.7 8.2 %all_gather.13 = bf16[1536,256]{1,0:T(8,128)(2,1)S(1)} all-gather(bf16[384,256]{1,0:T(8,128)(2,1)S(1)} %fusion.71), channel_id=1, replica_groups=mesh['groups'=2,'ctx'=4,'mp'=4] {'mp'}, dimensions={0}, use_global_device_ids=true | all-gather | bytes 983040 | tf_op jit(solution)/shard_map/all_gather | solution.py:39
  56.9 1.5 collective-permute-start.1
  58.8 1.5 reshape.35
  60.3 4.6 %all-to-all-start = ((bf16[4,2,12288]{2,1,0:T(2,128)(2,1)}), bf16[4,2,12288]{2,1,0:T(2,128)(2,1)}, u32[]{:S(2)}, u32[]{:S(2)}) async-start(bf16[4,2,12288]{2,1,0:T(2,128)(2,1)} %reshape.35), calls=%async_computation | async-start | bytes 393216 | tf_op jit(solution)/shard_map/all_to_all | solution.py:108
  64.9 1.4 fusion.23
  66.3 1.6 fusion.19
  68.0 1.6 fusion.16
  70.1 1.2 copy.35
  71.3 1.7 all-to-all-done
  73.0 1.4 reshape.36
  75.6 8.0 %all_gather.14 = bf16[1536,256]{1,0:T(8,128)(2,1)S(1)} all-gather(bf16[384,256]{1,0:T(8,128)(2,1)S(1)} %bitcast.104), channel_id=1, replica_groups=mesh['groups'=2,'ctx'=4,'mp'=4] {'mp'}, dimensions={0}, use_global_device_ids=true | all-gather | bytes 983040 | tf_op jit(solution)/shard_map/all_gather | solution.py:60
  86.1 1.2 copy.37
  87.3 1.7 fusion.12
  89.0 1.2 copy.47
  90.2 5.3 %reduce-scatter.27.cloned.1.call-done = bf16[384,256]{1,0:T(8,128)(2,1)} async-done(((bf16[1536,256]{1,0:T(8,128)(2,1)}), bf16[384,256]{1,0:T(8,128)(2,1)}) %reduce-scatter.27.cloned.1.call-update) | async-done | bytes 196624 | tf_op jit(solution)/shard_map/reduce_scatter | solution.py:46
  95.5 26.4 %reduce-scatter.29.cloned.1.call-done = bf16[384,256]{1,0:T(8,128)(2,1)} async-done(((bf16[1536,256]{1,0:T(8,128)(2,1)}), bf16[384,256]{1,0:T(8,128)(2,1)}) %reduce-scatter.29.cloned.1.call-update) | async-done | bytes 196624 | tf_op jit(solution)/shard_map/reduce_scatter | solution.py:76
  121.9 2.1 fusion.76
  124.1 8.2 %all_gather.15 = bf16[1536,256]{1,0:T(8,128)(2,1)S(1)} all-gather(bf16[384,256]{1,0:T(8,128)(2,1)S(1)} %get-tuple-element.24), channel_id=1, replica_groups=mesh['groups'=2,'ctx'=4,'mp'=4] {'mp'}, dimensions={0}, use_global_device_ids=true | all-gather | bytes 983040 | tf_op jit(solution)/shard_map/all_gather | solution.py:60
  132.3 1.2 convolution_convert_fusion.5
  133.5 2.2 copy.43
  135.8 1.5 fusion.88
  139.2 1.2 copy.39
  141.7 3.5 %copy.45 = bf16[3,192,1536]{1,0,2:T(4,128)(2,1)} copy(bf16[3,192,1536]{2,1,0:T(8,128)(2,1)S(1)} %pad_maximum_fusion.1) | data formatting | bytes 3538944
  145.3 7.0 %reshape.31 = bf16[1536,576]{1,0:T(8,128)(2,1)} reshape(bf16[1536,3,192]{2,1,0:T(4,128)(2,1)} %bitcast.98) | data formatting | bytes 3538944
  152.4 0.8 copy-done.16
  154.2 3.5 %copy.41 = bf16[3,192,1536]{1,0,2:T(4,128)(2,1)} copy(bf16[3,192,1536]{2,1,0:T(8,128)(2,1)S(1)} %pad_maximum_fusion) | data formatting | bytes 3538944
  157.8 7.1 %reshape.27 = bf16[1536,576]{1,0:T(8,128)(2,1)} reshape(bf16[1536,3,192]{2,1,0:T(4,128)(2,1)} %bitcast.99) | data formatting | bytes 3538944
  164.9 1.1 copy.48
  166.0 0.7 convert_element_type.137
  166.7 6.2 %reduce-scatter.35.cloned.1.call-done = bf16[384,192]{1,0:T(8,128)(2,1)} async-done(((bf16[1536,192]{1,0:T(8,128)(2,1)}), bf16[384,192]{1,0:T(8,128)(2,1)}) %reduce-scatter.35.cloned.1.call-update) | async-done | bytes 147472
  173.0 1.1 copy.44
  174.0 0.7 convert_element_type.133
  174.8 23.9 %reduce-scatter.31.cloned.1.call-done = bf16[384,256]{1,0:T(8,128)(2,1)} async-done(((bf16[1536,256]{1,0:T(8,128)(2,1)}), bf16[384,256]{1,0:T(8,128)(2,1)}) %reduce-scatter.31.cloned.1.call-update) | async-done | bytes 196624 | tf_op jit(solution)/shard_map/reduce_scatter | solution.py:76
  198.7 1.9 fusion.67
  200.6 41.9 %reduce-scatter.37.cloned.1.call-done = bf16[384,576]{1,0:T(8,128)(2,1)} async-done(((bf16[1536,576]{1,0:T(8,128)(2,1)}), bf16[384,576]{1,0:T(8,128)(2,1)}) %reduce-scatter.37.cloned.1.call-update) | async-done | bytes 442384
  242.5 1.8 reshape.32
  244.3 0.9 copy.46
  245.2 1.0 convert_element_type.134
  246.1 39.4 %reduce-scatter.33.cloned.1.call-done = bf16[384,576]{1,0:T(8,128)(2,1)} async-done(((bf16[1536,576]{1,0:T(8,128)(2,1)}), bf16[384,576]{1,0:T(8,128)(2,1)}) %reduce-scatter.33.cloned.1.call-update) | async-done | bytes 442384
  285.5 1.8 reshape.28
  287.3 0.9 copy.42
  288.2 1.0 convert_element_type.131
  (79 shorter events, 11.0 us)
Async XLA Ops:
  7.2 62.5 %copy-start = (bf16[1536,192]{0,1:T(8,128)(2,1)S(1)}, bf16[1536,192]{0,1:T(8,128)(2,1)}, u32[]{:S(2)}) copy-start(bf16[1536,192]{0,1:T(8,128)(2,1)} %param.10) | copy-start | bytes 1769476
  7.2 13.4 %copy-start.2 = (bf16[3,192,1536]{2,1,0:T(8,128)(2,1)S(1)}, bf16[3,192,1536]{2,1,0:T(8,128)(2,1)}, u32[]{:S(2)}) copy-start(bf16[3,192,1536]{2,1,0:T(8,128)(2,1)} %param.7) | copy-start | bytes 5308420
  7.2 40.4 %reduce-scatter.25.cloned.1.call-start = ((), (), s32[]{:S(2)}) async-start(), calls=%async_computation.9 | async-start | bytes 983040 | tf_op jit(solution)/shard_map/reduce_scatter | solution.py:46
  18.5 2.1 collective-permute-start
  20.6 1.1 copy-start.12
  21.7 25.9 %copy-start.5 = (bf16[384,256]{1,0:T(8,128)(2,1)S(1)}, bf16[384,256]{1,0:T(8,128)(2,1)}, u32[]{:S(2)}) copy-start(bf16[384,256]{1,0:T(8,128)(2,1)} %param.6) | copy-start | bytes 589828
  22.1 36.3 %copy-start.17 = (bf16[2,48,1024]{2,1,0:T(8,128)(2,1)S(1)}, bf16[2,48,1024]{2,1,0:T(8,128)(2,1)}, u32[]{:S(2)}) copy-start(bf16[2,48,1024]{2,1,0:T(8,128)(2,1)} %param.11) | copy-start | bytes 589828
  56.9 9.4 %collective-permute-start.1 = (bf16[1536,256]{1,0:T(8,128)(2,1)S(1)}, bf16[1536,256]{1,0:T(8,128)(2,1)}, u32[]{:S(2)}, u32[]{:S(2)}) collective-permute-start(bf16[1536,256]{1,0:T(8,128)(2,1)S(1)} %all_gather.13), channel_id=1, source_target_pairs={} | collective-permute-start | bytes 2359304 | tf_op jit(solution)/shard_map/ppermute | solution.py:13
  60.3 12.7 %all-to-all-start = ((bf16[4,2,12288]{2,1,0:T(2,128)(2,1)}), bf16[4,2,12288]{2,1,0:T(2,128)(2,1)}, u32[]{:S(2)}, u32[]{:S(2)}) async-start(bf16[4,2,12288]{2,1,0:T(2,128)(2,1)} %reshape.35), calls=%async_computation | async-start | bytes 393216 | tf_op jit(solution)/shard_map/all_to_all | solution.py:108
  64.9 30.6 %reduce-scatter.27.cloned.1.call-start = ((), (), s32[]{:S(2)}) async-start(), calls=%async_computation.10 | async-start | bytes 983040 | tf_op jit(solution)/shard_map/reduce_scatter | solution.py:46
  71.2 50.7 %reduce-scatter.29.cloned.1.call-start = ((), (), s32[]{:S(2)}) async-start(), calls=%async_computation.11 | async-start | bytes 983040 | tf_op jit(solution)/shard_map/reduce_scatter | solution.py:76
  74.9 9.7 %copy-start.1 = (bf16[3,192,1536]{2,1,0:T(8,128)(2,1)S(1)}, bf16[3,192,1536]{2,1,0:T(8,128)(2,1)}, u32[]{:S(2)}) copy-start(bf16[3,192,1536]{2,1,0:T(8,128)(2,1)} %param.9) | copy-start | bytes 5308420
  74.9 0.7 copy-start.8
  83.6 1.4 copy-start.4
  83.9 1.1 copy-start.13
  83.9 1.1 collective-permute-start.2
  85.0 0.6 copy-start.10
  87.3 34.7 %copy-start.9 = (bf16[2,4,48,256]{3,2,1,0:T(8,128)(2,1)S(1)}, bf16[2,4,48,256]{3,2,1,0:T(8,128)(2,1)}, u32[]{:S(2)}) copy-start(bf16[2,4,48,256]{3,2,1,0:T(8,128)(2,1)} %copy-done.8) | copy-start | bytes 589828
  87.3 77.6 %reduce-scatter.39.cloned.1.call-start = ((), (), s32[]{:S(2)}) async-start(), calls=%async_computation.16 | async-start | bytes 983040
  90.2 82.8 %reduce-scatter.35.cloned.1.call-start = ((), (), s32[]{:S(2)}) async-start(), calls=%async_computation.14 | async-start | bytes 983040
  124.1 11.7 %copy-start.6 = (bf16[384,256]{1,0:T(8,128)(2,1)}, bf16[384,256]{1,0:T(8,128)(2,1)S(1)}, u32[]{:S(2)}) copy-start(bf16[384,256]{1,0:T(8,128)(2,1)S(1)} %get-tuple-element.24) | copy-start | bytes 589828
  135.7 62.9 %reduce-scatter.31.cloned.1.call-start = ((), (), s32[]{:S(2)}) async-start(), calls=%async_computation.12 | async-start | bytes 983040 | tf_op jit(solution)/shard_map/reduce_scatter | solution.py:76
  135.8 2.2 copy-start.3
  137.3 1.5 copy-start.15
  137.3 1.1 collective-permute-start.3
  139.2 1.4 copy-start.14
  139.2 1.9 copy-start.11
  140.4 102.1 %reduce-scatter.37.cloned.1.call-start = ((), (), s32[]{:S(2)}) async-start(), calls=%async_computation.15 | async-start | bytes 2457600
  152.3 0.9 copy-start.16
  152.3 133.2 %reduce-scatter.33.cloned.1.call-start = ((), (), s32[]{:S(2)}) async-start(), calls=%async_computation.13 | async-start | bytes 2457600
  164.8 33.8 %copy-start.7 = (bf16[384,256]{1,0:T(8,128)(2,1)S(1)}, bf16[384,256]{1,0:T(8,128)(2,1)}, u32[]{:S(2)}) copy-start(bf16[384,256]{1,0:T(8,128)(2,1)} %copy-done.6) | copy-start | bytes 589828
Sparse Core Ops, SparseCore 0:
  23.4 24.1 reduce-scatter.24
  71.4 24.1 reduce-scatter.26
  98.6 23.2 reduce-scatter.28
  124.2 23.3 reduce-scatter.38
  150.4 22.5 reduce-scatter.34
  176.1 22.5 reduce-scatter.30
  201.0 41.4 reduce-scatter.36
  244.8 40.6 reduce-scatter.32
where the time goes:
time: 297 us; the launch traced here: 296 us
  waiting for transfers between devices  169 us (57%)
  local copies, waits for them, and re-layouts  42.7 us (14%)
  blocking collectives  34.5 us (12%)
  matrix products  16.2 us (5%)
  between operations  14.6 us (5%)
  other arithmetic  10.2 us (3%)
  starting transfers between devices  8.6 us (3%)
    unnamed x12, waiting for transfers between devices  87.6 us
    reduce_scatter x2, waiting for transfers between devices, residual_block_backward(): lax.psum_scatter((total + contract_first(conv_weight[2], moved[2])).astyp...  50.3 us
    unnamed x55, local copies, waits for them, and re-layouts  42.3 us
    reduce_scatter x2, waiting for transfers between devices, residual_block_forward(): lax.psum_scatter(jnp.dot(point_weight, hidden, preferred_element_type=jnp...  29.6 us
    all_gather x2, blocking collectives, residual_block_forward(): squashed = lax.all_gather(squash_part, 'mp', axis=0, tiled=True)  18.3 us
    all_gather x2, blocking collectives, residual_block_backward(): upstream_full = lax.all_gather(incoming_gradient, 'mp', axis=0, tiled=True)  16.2 us
  transfers between devices with their start and end apart: 13, of which 8 were waited for; matrix products, arithmetic and copies ran while one was open for 20% of the time, Pallas kernels for 0%

commit v1 on v0

--- a/solution.py
+++ b/solution.py
@@ -105,7 +105,10 @@
     second_pointwise_weight,
     grad_heads,
 ):
-    regrouped = lax.all_to_all(grad_heads, "ctx", split_axis=2, concat_axis=1, tiled=True)
+    regrouped = jnp.concatenate(
+        lax.all_to_all(jnp.stack(jnp.split(grad_heads, lax.axis_size("ctx"), axis=2)), "ctx", 0, 0),
+        axis=1,
+    )
     incoming_gradient = regrouped.reshape(
         regrouped.shape[0] * regrouped.shape[1], regrouped.shape[2]
     )

time: 297 us -> 296 us (level)
    unnamed x55 -> x50, local copies, waits for them, and re-layouts: 42.3 us -> 38.8 us
  transfers between devices with their start and end apart: 13 -> 13, of which waited for: 8 -> 8; matrix products, arithmetic and copies ran while one was open for 20% -> 19% of each run, Pallas kernels for 0% -> 0%
where the time goes in v1:
time: 296 us; the launch traced here: 294 us
  waiting for transfers between devices  170 us (57%)
  local copies, waits for them, and re-layouts  40.7 us (14%)
  blocking collectives  34.4 us (12%)
  matrix products  15.7 us (5%)
  between operations  14.6 us (5%)
  other arithmetic  10.9 us (4%)
  starting transfers between devices  7.77 us (3%)
    unnamed x12, waiting for transfers between devices  87.8 us
    reduce_scatter x2, waiting for transfers between devices, residual_block_backward(): lax.psum_scatter((total + contract_first(conv_weight[2], moved[2])).astyp...  50.3 us
    unnamed x50, local copies, waits for them, and re-layouts  38.8 us
    reduce_scatter x2, waiting for transfers between devices, residual_block_forward(): lax.psum_scatter(jnp.dot(point_weight, hidden, preferred_element_type=jnp...  30 us
    all_gather x2, blocking collectives, residual_block_forward(): squashed = lax.all_gather(squash_part, 'mp', axis=0, tiled=True)  18.3 us
    all_gather x2, blocking collectives, residual_block_backward(): upstream_full = lax.all_gather(incoming_gradient, 'mp', axis=0, tiled=True)  16.2 us
  transfers between devices with their start and end apart: 13, of which 8 were waited for; matrix products, arithmetic and copies ran while one was open for 19% of the time, Pallas kernels for 0%

profile of v1, /device:TPU:0, one launch (start us, length us, event | category | flops | bytes accessed | tf_op | source)
XLA Modules:
  0.0 294.4 jit_solution(13335595561705027763)
XLA Ops:
  7.2 1.2 fusion.61
  8.5 10.0 %all_gather.12 = bf16[1536,256]{1,0:T(8,128)(2,1)S(1)} all-gather(bf16[384,256]{1,0:T(8,128)(2,1)S(1)} %fusion.61), channel_id=1, replica_groups=mesh['groups'=2,'ctx'=4,'mp'=4] {'mp'}, dimensions={0}, use_global_device_ids=true | all-gather | bytes 983040 | tf_op jit(solution)/shard_map/all_gather | solution.py:39
  18.5 0.7 collective-permute-start
  19.2 1.4 fusion.32
  22.1 1.2 copy.25
  23.3 24.3 %reduce-scatter.25.cloned.1.call-done = bf16[384,256]{1,0:T(8,128)(2,1)} async-done(((bf16[1536,256]{1,0:T(8,128)(2,1)}), bf16[384,256]{1,0:T(8,128)(2,1)}) %reduce-scatter.25.cloned.1.call-update) | async-done | bytes 196624 | tf_op jit(solution)/shard_map/reduce_scatter | solution.py:46
  47.6 1.1 fusion.70
  48.7 8.2 %all_gather.13 = bf16[1536,256]{1,0:T(8,128)(2,1)S(1)} all-gather(bf16[384,256]{1,0:T(8,128)(2,1)S(1)} %fusion.70), channel_id=1, replica_groups=mesh['groups'=2,'ctx'=4,'mp'=4] {'mp'}, dimensions={0}, use_global_device_ids=true | all-gather | bytes 983040 | tf_op jit(solution)/shard_map/all_gather | solution.py:39
  57.6 0.9 slice_bitcast_fusion.3
  58.5 0.7 pad_maximum_fusion.2
  59.2 4.6 %all-to-all-start = ((bf16[4,2,48,256]{3,2,1,0:T(8,128)(2,1)}), bf16[4,2,48,256]{3,2,1,0:T(8,128)(2,1)}, u32[]{:S(2)}, u32[]{:S(2)}) async-start(bf16[4,2,48,256]{3,2,1,0:T(8,128)(2,1)} %pad_maximum_fusion.2), calls=%async_computation | async-start | bytes 393216 | tf_op jit(solution)/shard_map/all_to_all | solution.py:109
  63.8 1.4 fusion.22
  65.2 1.4 fusion.18
  66.6 1.4 fusion.15
  68.4 1.2 copy.27
  69.6 2.2 all-to-all-done
  71.9 1.1 copy.22
  73.6 8.0 %all_gather.14 = bf16[1536,256]{1,0:T(8,128)(2,1)S(1)} all-gather(bf16[384,256]{1,0:T(8,128)(2,1)S(1)} %bitcast.108), channel_id=1, replica_groups=mesh['groups'=2,'ctx'=4,'mp'=4] {'mp'}, dimensions={0}, use_global_device_ids=true | all-gather | bytes 983040 | tf_op jit(solution)/shard_map/all_gather | solution.py:60
  84.1 1.2 copy.29
  85.3 1.6 convolution_convert_fusion.2
  86.9 1.2 copy.39
  88.2 5.7 %reduce-scatter.27.cloned.1.call-done = bf16[384,256]{1,0:T(8,128)(2,1)} async-done(((bf16[1536,256]{1,0:T(8,128)(2,1)}), bf16[384,256]{1,0:T(8,128)(2,1)}) %reduce-scatter.27.cloned.1.call-update) | async-done | bytes 196624 | tf_op jit(solution)/shard_map/reduce_scatter | solution.py:46
  93.9 26.4 %reduce-scatter.29.cloned.1.call-done = bf16[384,256]{1,0:T(8,128)(2,1)} async-done(((bf16[1536,256]{1,0:T(8,128)(2,1)}), bf16[384,256]{1,0:T(8,128)(2,1)}) %reduce-scatter.29.cloned.1.call-update) | async-done | bytes 196624 | tf_op jit(solution)/shard_map/reduce_scatter | solution.py:76
  120.3 2.1 fusion.75
  122.5 8.2 %all_gather.15 = bf16[1536,256]{1,0:T(8,128)(2,1)S(1)} all-gather(bf16[384,256]{1,0:T(8,128)(2,1)S(1)} %get-tuple-element.18), channel_id=1, replica_groups=mesh['groups'=2,'ctx'=4,'mp'=4] {'mp'}, dimensions={0}, use_global_device_ids=true | all-gather | bytes 983040 | tf_op jit(solution)/shard_map/all_gather | solution.py:60
  130.6 1.2 convolution_convert_fusion.5
  131.9 2.2 copy.35
  134.2 1.5 fusion.87
  137.6 1.2 copy.31
  139.9 3.5 %copy.37 = bf16[3,192,1536]{1,0,2:T(4,128)(2,1)} copy(bf16[3,192,1536]{2,1,0:T(8,128)(2,1)S(1)} %pad_maximum_fusion.1) | data formatting | bytes 3538944
  143.4 7.0 %reshape.30 = bf16[1536,576]{1,0:T(8,128)(2,1)} reshape(bf16[1536,3,192]{2,1,0:T(4,128)(2,1)} %bitcast.104) | data formatting | bytes 3538944
  152.4 3.5 %copy.33 = bf16[3,192,1536]{1,0,2:T(4,128)(2,1)} copy(bf16[3,192,1536]{2,1,0:T(8,128)(2,1)S(1)} %pad_maximum_fusion) | data formatting | bytes 3538944
  156.0 7.1 %reshape.26 = bf16[1536,576]{1,0:T(8,128)(2,1)} reshape(bf16[1536,3,192]{2,1,0:T(4,128)(2,1)} %bitcast.105) | data formatting | bytes 3538944
  163.1 1.1 copy.40
  164.2 0.7 convert_element_type.133
  164.9 6.4 %reduce-scatter.35.cloned.1.call-done = bf16[384,192]{1,0:T(8,128)(2,1)} async-done(((bf16[1536,192]{1,0:T(8,128)(2,1)}), bf16[384,192]{1,0:T(8,128)(2,1)}) %reduce-scatter.35.cloned.1.call-update) | async-done | bytes 147472
  171.3 1.1 copy.36
  172.4 0.7 convert_element_type.130
  173.2 23.9 %reduce-scatter.31.cloned.1.call-done = bf16[384,256]{1,0:T(8,128)(2,1)} async-done(((bf16[1536,256]{1,0:T(8,128)(2,1)}), bf16[384,256]{1,0:T(8,128)(2,1)}) %reduce-scatter.31.cloned.1.call-update) | async-done | bytes 196624 | tf_op jit(solution)/shard_map/reduce_scatter | solution.py:76
  197.0 1.9 fusion.66
  198.9 41.9 %reduce-scatter.37.cloned.1.call-done = bf16[384,576]{1,0:T(8,128)(2,1)} async-done(((bf16[1536,576]{1,0:T(8,128)(2,1)}), bf16[384,576]{1,0:T(8,128)(2,1)}) %reduce-scatter.37.cloned.1.call-update) | async-done | bytes 442384
  240.8 1.8 reshape.31
  242.6 0.9 copy.38
  243.5 1.0 convert_element_type.131
  244.5 39.3 %reduce-scatter.33.cloned.1.call-done = bf16[384,576]{1,0:T(8,128)(2,1)} async-done(((bf16[1536,576]{1,0:T(8,128)(2,1)}), bf16[384,576]{1,0:T(8,128)(2,1)}) %reduce-scatter.33.cloned.1.call-update) | async-done | bytes 442384
  283.8 1.8 reshape.27
  285.7 0.9 copy.34
  286.6 1.0 convert_element_type.128
  (75 shorter events, 10.8 us)
Async XLA Ops:
  7.2 60.8 %copy-start = (bf16[1536,192]{0,1:T(8,128)(2,1)S(1)}, bf16[1536,192]{0,1:T(8,128)(2,1)}, u32[]{:S(2)}) copy-start(bf16[1536,192]{0,1:T(8,128)(2,1)} %param.10) | copy-start | bytes 1769476
  7.2 13.4 %copy-start.2 = (bf16[3,192,1536]{2,1,0:T(8,128)(2,1)S(1)}, bf16[3,192,1536]{2,1,0:T(8,128)(2,1)}, u32[]{:S(2)}) copy-start(bf16[3,192,1536]{2,1,0:T(8,128)(2,1)} %param.7) | copy-start | bytes 5308420
  7.2 40.4 %reduce-scatter.25.cloned.1.call-start = ((), (), s32[]{:S(2)}) async-start(), calls=%async_computation.9 | async-start | bytes 983040 | tf_op jit(solution)/shard_map/reduce_scatter | solution.py:46
  18.5 2.1 collective-permute-start
  20.6 1.1 copy-start.12
  21.7 25.9 %copy-start.5 = (bf16[384,256]{1,0:T(8,128)(2,1)S(1)}, bf16[384,256]{1,0:T(8,128)(2,1)}, u32[]{:S(2)}) copy-start(bf16[384,256]{1,0:T(8,128)(2,1)} %param.6) | copy-start | bytes 589828
  56.9 8.3 %collective-permute-start.1 = (bf16[1536,256]{1,0:T(8,128)(2,1)S(1)}, bf16[1536,256]{1,0:T(8,128)(2,1)S(1)}, u32[]{:S(2)}, u32[]{:S(2)}) collective-permute-start(bf16[1536,256]{1,0:T(8,128)(2,1)S(1)} %all_gather.13), channel_id=1, source_target_pairs={} | collective-permute-start | bytes 2359304 | tf_op jit(solution)/shard_map/ppermute | solution.py:13
  59.2 12.7 %all-to-all-start = ((bf16[4,2,48,256]{3,2,1,0:T(8,128)(2,1)}), bf16[4,2,48,256]{3,2,1,0:T(8,128)(2,1)}, u32[]{:S(2)}, u32[]{:S(2)}) async-start(bf16[4,2,48,256]{3,2,1,0:T(8,128)(2,1)} %pad_maximum_fusion.2), calls=%async_computation | async-start | bytes 393216 | tf_op jit(solution)/shard_map/all_to_all | solution.py:109
  63.8 30.1 %reduce-scatter.27.cloned.1.call-start = ((), (), s32[]{:S(2)}) async-start(), calls=%async_computation.10 | async-start | bytes 983040 | tf_op jit(solution)/shard_map/reduce_scatter | solution.py:46
  69.6 50.7 %reduce-scatter.29.cloned.1.call-start = ((), (), s32[]{:S(2)}) async-start(), calls=%async_computation.11 | async-start | bytes 983040 | tf_op jit(solution)/shard_map/reduce_scatter | solution.py:76
  71.9 10.8 %copy-start.1 = (bf16[3,192,1536]{2,1,0:T(8,128)(2,1)S(1)}, bf16[3,192,1536]{2,1,0:T(8,128)(2,1)}, u32[]{:S(2)}) copy-start(bf16[3,192,1536]{2,1,0:T(8,128)(2,1)} %param.9) | copy-start | bytes 5308420
  72.9 0.7 copy-start.8
  81.6 1.4 copy-start.4
  82.0 1.1 copy-start.13
  82.0 1.1 collective-permute-start.2
  83.1 0.6 copy-start.10
  85.3 35.0 %copy-start.9 = (bf16[4,2,48,256]{3,2,0,1:T(8,128)(2,1)S(1)}, bf16[4,2,48,256]{3,2,0,1:T(8,128)(2,1)}, u32[]{:S(2)}) copy-start(bf16[4,2,48,256]{3,2,0,1:T(8,128)(2,1)} %copy-done.8) | copy-start | bytes 589828
  85.3 77.8 %reduce-scatter.39.cloned.1.call-start = ((), (), s32[]{:S(2)}) async-start(), calls=%async_computation.16 | async-start | bytes 983040
  88.1 83.2 %reduce-scatter.35.cloned.1.call-start = ((), (), s32[]{:S(2)}) async-start(), calls=%async_computation.14 | async-start | bytes 983040
  122.5 11.6 %copy-start.6 = (bf16[384,256]{1,0:T(8,128)(2,1)}, bf16[384,256]{1,0:T(8,128)(2,1)S(1)}, u32[]{:S(2)}) copy-start(bf16[384,256]{1,0:T(8,128)(2,1)S(1)} %get-tuple-element.18) | copy-start | bytes 589828
  134.1 62.9 %reduce-scatter.31.cloned.1.call-start = ((), (), s32[]{:S(2)}) async-start(), calls=%async_computation.12 | async-start | bytes 983040 | tf_op jit(solution)/shard_map/reduce_scatter | solution.py:76
  134.1 2.2 copy-start.3
  135.7 1.5 copy-start.15
  135.7 1.1 collective-permute-start.3
  137.6 1.3 copy-start.14
  137.6 1.7 copy-start.11
  138.8 102.1 %reduce-scatter.37.cloned.1.call-start = ((), (), s32[]{:S(2)}) async-start(), calls=%async_computation.15 | async-start | bytes 2457600
  150.5 0.9 copy-start.16
  150.5 133.3 %reduce-scatter.33.cloned.1.call-start = ((), (), s32[]{:S(2)}) async-start(), calls=%async_computation.13 | async-start | bytes 2457600
  163.0 34.0 %copy-start.7 = (bf16[384,256]{1,0:T(8,128)(2,1)S(1)}, bf16[384,256]{1,0:T(8,128)(2,1)}, u32[]{:S(2)}) copy-start(bf16[384,256]{1,0:T(8,128)(2,1)} %copy-done.6) | copy-start | bytes 589828
Sparse Core Ops, SparseCore 0:
  23.4 24.1 reduce-scatter.24
  69.7 24.1 reduce-scatter.26
  97.0 23.2 reduce-scatter.28
  122.6 23.3 reduce-scatter.38
  148.8 22.5 reduce-scatter.34
  174.5 22.4 reduce-scatter.30
  199.3 41.4 reduce-scatter.36
  243.1 40.6 reduce-scatter.32
